TPU v7x, 256 devices: a whole 4x4x8 slice. The times are simulated.
256 devices in a mesh: row: 8 (over x, core), col: 32 (over z, y).
Axes of the slice: x: 4, y: 4, z: 8, core: 2. Of those that a mesh axis runs over, the one named last changes fastest.
Arguments:
- layer_input: bfloat16 [16896, 1024], P('col', 'row'), may hold values from -6 to 6
- w_q: bfloat16 [1024, 1024], P('col', 'row'), may hold values from -0.1875 to 0.1875
- w_k: bfloat16 [1024, 1024], P('col', 'row'), may hold values from -0.1875 to 0.1875
- w_v: bfloat16 [1024, 1024], P('col', 'row'), may hold values from -0.1875 to 0.1875
- w_o: bfloat16 [1024, 1024], P('row', 'col'), may hold values from -0.375 to 0.375
- w_gate: bfloat16 [1024, 4096], P('col', 'row'), may hold values from -0.1875 to 0.1875
- w_up: bfloat16 [1024, 4096], P('col', 'row'), may hold values from -0.1875 to 0.1875
- w_down: bfloat16 [4096, 1024], P('row', 'col'), may hold values from -0.1875 to 0.1875
- norm1: float32 [1024], replicated, may hold values from 0.5 to 1.5
- norm2: float32 [1024], replicated, may hold values from 0.5 to 1.5
- q_gain: float32 [1024], P('row'), may hold values from 0.5 to 1.5
- k_gain: float32 [1024], P('row'), may hold values from 0.5 to 1.5
- bias_same: float32 [16], P('row'), may hold values from -3 to 3
- bias_diff: float32 [16], P('row'), may hold values from -3 to 3
- pre_variate: int32 [32, 512], P('col'), may hold values from 0 to 7, never falling along the last dimension, each value on 1 to 128 neighbouring positions
- pre_keep: int32 [32, 512], P('col'), may hold values 0 or 1
- dec_variate: int32 [512], P('col'), may hold values from 0 to 7
- dec_len: int32 [512], P('col'), may hold values from 1 to 1023, as said below
- dec_table: int32 [512, 8], P('col'), may hold values from 0 to 31
- dec_holder: int32 [512, 1], P('col'), may hold values from 0 to 31; in each aligned block of 16 rows (0 to 15, 16 to 31, ...) at most 2 rows name the same one
- kv_pool: bfloat16 [1024, 2, 128, 1024], P('col', None, None, 'row'), may hold values from -4 to 4
- page_variates: int32 [1024, 128], P('col'), may hold values from 0 to 7
Outputs:
- hidden: bfloat16 [16896, 1024], P('col', 'row')
- prefill_pages: bfloat16 [128, 2, 128, 1024], P('col', None, None, 'row')
- tail_pages: bfloat16 [512, 2, 128, 1024], P('col', None, None, 'row')
Inputs may be any that keep to these rules, and one draw needn't show every extreme that they name: `pre_variate`: each variate's tokens form one run of at most 128 positions. `dec_len`: some request has exactly 1023 cached tokens. `dec_table`: entries past a request's last page are unused; requests may share pages. `dec_holder`: among the 16 requests of one column group at most 2 name the same holder, a bound that some block reaches of them.
All inputs are finite; a program needn't handle non-finite values. No bound on the sum of `pre_keep` on one device may be relied on, other than what follows from the above.
Results may differ from a plain program's by a relative error of at most 0.015.
Values may be sent and summed in bfloat16 or wider, within the bound.
No kernel may reach another device: no remote copies, remote signals or barrier semaphores. Data moves between devices by JAX's collectives and lax.ppermute only.
A program may use at most 128 MiB of HBM per device.

v0:
```python
import jax
import jax.numpy as jnp
from jax import lax
from jax.sharding import PartitionSpec as P

HD = 64
eps = 1e-05


def as_sent(array):
    return jax.tree.map(lambda a: a.astype(jnp.bfloat16) if a.dtype == jnp.float32 else a, array)


def norm_rows(values, gain_row):
    return values * lax.rsqrt(jnp.mean(values * values, axis=-1, keepdims=True) + eps) * gain_row


def rotate(tensor, places):
    half_size = tensor.shape[-1] // 2
    spacing = jnp.arange(half_size).astype(jnp.float32) * (2.0 / tensor.shape[-1])
    angles = places.astype(jnp.float32)[:, None] * jnp.power(10000.0, -spacing)[None, :]
    cosine = jnp.cos(angles)[:, None, :]
    sine_part = jnp.sin(angles)[:, None, :]
    lower_half = tensor[..., :half_size]
    upper_half = tensor[..., half_size:]
    return jnp.concatenate(
        [
            lower_half * cosine - upper_half * sine_part,
            upper_half * cosine + lower_half * sine_part,
        ],
        axis=-1,
    )


def segment_time(variates):
    places = jnp.arange(variates.shape[0])
    run_start = jnp.concatenate([jnp.ones((1,), dtype=jnp.bool_), variates[1:] != variates[:-1]])
    starts = lax.cummax(jnp.where(run_start, places, 0), axis=0)
    return places - starts


def on_device(
    layer_input,
    w_q,
    w_k,
    w_v,
    w_o,
    w_gate,
    w_up,
    w_down,
    norm1,
    norm2,
    q_gain,
    k_gain,
    bias_same,
    bias_diff,
    pre_variate,
    pre_keep,
    dec_variate,
    dec_len,
    dec_table,
    dec_holder,
    kv_pool,
    page_variates,
):
    row_count = layer_input.shape[0]
    local_width = layer_input.shape[1]
    pre_len = pre_variate.shape[1]
    dec_count = dec_len.shape[0]
    heads_here = local_width // HD
    score_scale = HD ** (-0.5)
    page_size = kv_pool.shape[2]
    page_count = dec_table.shape[1]
    gathered_input = lax.all_gather(layer_input, "row", axis=1, tiled=True)
    normed = norm_rows(gathered_input.astype(jnp.float32), norm1).astype(jnp.bfloat16)
    pieces = (
        lax.all_gather(w_q, "col", axis=0, tiled=True),
        lax.all_gather(w_k, "col", axis=0, tiled=True),
        lax.all_gather(w_v, "col", axis=0, tiled=True),
    )
    columns = normed
    queries = jnp.dot(columns, pieces[0], preferred_element_type=jnp.float32)
    keys_proj = jnp.dot(columns, pieces[1], preferred_element_type=jnp.float32)
    values_proj = jnp.dot(columns, pieces[2], preferred_element_type=jnp.float32)
    places = jnp.concatenate([segment_time(pre_variate[0]), dec_len])
    query_rot = rotate(
        norm_rows(queries.reshape(row_count, heads_here, HD), q_gain.reshape(heads_here, HD)),
        places,
    ).astype(jnp.bfloat16)
    key_rot = rotate(
        norm_rows(keys_proj.reshape(row_count, heads_here, HD), k_gain.reshape(heads_here, HD)),
        places,
    ).astype(jnp.bfloat16)
    value_bf = values_proj.astype(jnp.bfloat16).reshape(row_count, heads_here, HD)

    def attend_slot(inputs):
        float_item, int_item = inputs
        new_query = float_item[:local_width].reshape(heads_here, HD)
        new_key = float_item[local_width : 2 * local_width]
        new_value = float_item[2 * local_width :]
        page_rows = int_item[:page_count]
        length = int_item[page_count]
        variate = int_item[page_count + 1]
        gathered = kv_pool[page_rows]
        cached_keys = gathered[:, 0].reshape(page_count * page_size, heads_here, HD)
        cached_vals = gathered[:, 1].reshape(page_count * page_size, heads_here, HD)
        key_variates = page_variates[page_rows].reshape(page_count * page_size)
        scores = (
            jnp.einsum("hd,khd->hk", new_query, cached_keys, preferred_element_type=jnp.float32)
            * score_scale
        )
        scores = scores + jnp.where(
            (key_variates == variate)[None, :], bias_same[:, None], bias_diff[:, None]
        )
        key_heads = new_key.reshape(heads_here, HD)
        value_heads = new_value.reshape(heads_here, HD)
        own_score = (
            jnp.sum(new_query.astype(jnp.float32) * key_heads.astype(jnp.float32), axis=1)
            * score_scale
            + bias_same
        )
        exp_scores = jnp.where(
            (jnp.arange(page_count * page_size) < length)[None, :], jnp.exp(scores), 0.0
        )
        own_exp = jnp.exp(own_score)
        total_weight = jnp.sum(exp_scores, axis=1) + own_exp
        weights_bf = (exp_scores / total_weight[:, None]).astype(jnp.bfloat16)
        own_weight = (own_exp / total_weight).astype(jnp.bfloat16)
        attended = jnp.einsum(
            "hk,khd->hd", weights_bf, cached_vals, preferred_element_type=jnp.float32
        ) + own_weight.astype(jnp.float32)[:, None] * value_heads.astype(jnp.float32)
        tail_slot = page_rows[length // page_size]
        old_page = kv_pool[tail_slot]
        hit_row = (jnp.arange(page_size) == length % page_size)[None, :, None]
        new_rows = jnp.stack([new_key, new_value])[:, None, :]
        return (
            attended.astype(jnp.bfloat16).reshape(local_width),
            jnp.where(hit_row, new_rows, old_page),
        )

    keep_mask = pre_keep[0]
    variates = pre_variate[0]
    block_rows = min(512, pre_len)
    pre_keys = key_rot[:pre_len]
    pre_values = value_bf[:pre_len]
    block_queries = query_rot[0:block_rows]
    scores = (
        jnp.einsum("qhd,khd->hqk", block_queries, pre_keys, preferred_element_type=jnp.float32)
        * score_scale
    )
    same_var = variates[0:block_rows, None] == variates[None, :]
    scores = scores + jnp.where(same_var[None], bias_same[:, None, None], bias_diff[:, None, None])
    allowed = (keep_mask[None, :] == 1) | (
        jnp.arange(0, block_rows)[:, None] == jnp.arange(pre_len)[None, :]
    )
    exp_scores = jnp.where(allowed[None], jnp.exp(scores), 0.0)
    weights_bf = (exp_scores / jnp.sum(exp_scores, axis=2, keepdims=True)).astype(jnp.bfloat16)
    outputs = jnp.einsum(
        "hqk,khd->qhd", weights_bf, pre_values, preferred_element_type=jnp.float32
    ).astype(jnp.bfloat16)
    prefill_out = outputs.reshape(pre_len, local_width)
    peer_count = lax.axis_size("col")
    slot_count = max(2, (dec_count + peer_count - 1) // peer_count)
    holder = dec_holder[:, 0]
    onehot = (holder[:, None] == jnp.arange(peer_count)[None, :]).astype(jnp.int32)
    slot_rank = jnp.sum((jnp.cumsum(onehot, axis=0) - onehot) * onehot, axis=1)
    target = holder * slot_count + slot_rank
    payload = jnp.concatenate(
        [
            query_rot[pre_len:].reshape(dec_count, local_width),
            key_rot[pre_len:].reshape(dec_count, local_width),
            value_bf[pre_len:].reshape(dec_count, local_width),
        ],
        axis=1,
    )
    int_facts = jnp.concatenate([dec_table, dec_len[:, None], dec_variate[:, None]], axis=1)
    send_float = (
        jnp.zeros((peer_count * slot_count, 3 * local_width), jnp.bfloat16).at[target].set(payload)
    )
    send_int = (
        jnp.zeros((peer_count * slot_count, page_count + 2), jnp.int32).at[target].set(int_facts)
    )
    send_float = send_float.reshape(peer_count, slot_count, 3 * local_width)
    send_int = send_int.reshape(peer_count, slot_count, page_count + 2)
    floats = lax.all_to_all(send_float, "col", split_axis=0, concat_axis=0, tiled=True)
    int_part = lax.all_to_all(send_int, "col", split_axis=0, concat_axis=0, tiled=True)
    group_count = floats.shape[0]
    item_count = floats.shape[1]
    flat_floats = floats.reshape(group_count * item_count, floats.shape[2])
    flat_ints = int_part.reshape(group_count * item_count, int_part.shape[2])
    batch_slots = min(16, group_count * item_count)
    slot_out, slot_tail = lax.map(attend_slot, (flat_floats, flat_ints), batch_size=batch_slots)
    slot_out = slot_out.reshape(group_count, item_count, local_width)
    slot_tail = slot_tail.reshape(group_count, item_count, 2, page_size, local_width)
    back_out = lax.all_to_all(
        as_sent(slot_out), "col", split_axis=0, concat_axis=0, tiled=True
    ).astype(slot_out.dtype)
    back_tail = lax.all_to_all(
        as_sent(slot_tail), "col", split_axis=0, concat_axis=0, tiled=True
    ).astype(slot_tail.dtype)
    decode_out = back_out.reshape(peer_count * slot_count, local_width)[target]
    tails = back_tail.reshape(peer_count * slot_count, 2, page_size, local_width)[target]
    decode_out, tail_pages = (decode_out, tails)
    all_attended = jnp.concatenate([prefill_out, decode_out], axis=0)
    partial_out = jnp.dot(
        all_attended,
        lax.all_gather(w_o, "col", axis=1, tiled=True),
        preferred_element_type=jnp.float32,
    )
    share_start = lax.axis_index("row") * local_width
    attn_total = lax.psum(partial_out.astype(jnp.bfloat16), "row").astype(jnp.float32)
    resid_full = gathered_input.astype(jnp.float32) + attn_total
    ffn_input = norm_rows(resid_full, norm2).astype(jnp.bfloat16)
    resid_share = lax.dynamic_slice_in_dim(resid_full, share_start, local_width, 1)
    zero_hidden = jnp.zeros((row_count, w_gate.shape[1]), jnp.float32)
    pieces = (
        lax.all_gather(w_gate, "col", axis=0, tiled=True),
        lax.all_gather(w_up, "col", axis=0, tiled=True),
    )
    columns = lax.slice_in_dim(ffn_input, 0, pieces[0].shape[0], axis=1)
    gate_proj = zero_hidden + jnp.dot(columns, pieces[0], preferred_element_type=jnp.float32)
    up_proj = zero_hidden + jnp.dot(columns, pieces[1], preferred_element_type=jnp.float32)
    hidden_units = (jax.nn.silu(gate_proj) * up_proj).astype(jnp.bfloat16)
    partial_ffn = jnp.dot(
        hidden_units,
        lax.all_gather(w_down, "col", axis=1, tiled=True),
        preferred_element_type=jnp.float32,
    )
    ffn_share = lax.psum_scatter(
        partial_ffn.astype(jnp.bfloat16), "row", scatter_dimension=1, tiled=True
    ).astype(jnp.float32)
    hidden = (resid_share + ffn_share).astype(jnp.bfloat16)
    prefill_pages = jnp.stack(
        [
            key_rot[:pre_len].reshape(pre_len // page_size, page_size, local_width),
            value_bf[:pre_len].reshape(pre_len // page_size, page_size, local_width),
        ],
        axis=1,
    )
    return (hidden, prefill_pages, tail_pages)


def solution(mesh):
    placed = (
        P("col", "row"),
        P("col", "row"),
        P("col", "row"),
        P("col", "row"),
        P("row", "col"),
        P("col", "row"),
        P("col", "row"),
        P("row", "col"),
        P(),
        P(),
        P("row"),
        P("row"),
        P("row"),
        P("row"),
        P("col", None),
        P("col", None),
        P("col"),
        P("col"),
        P("col", None),
        P("col", None),
        P("col", None, None, "row"),
        P("col", None),
    )
    return jax.shard_map(
        on_device,
        mesh=mesh,
        in_specs=placed,
        out_specs=(P("col", "row"), P("col", None, None, "row"), P("col", None, None, "row")),
        check_vma=False,
    )
```

profile of v0, /device:TPU:8, one launch (start us, length us, event | category | flops | bytes accessed | tf_op | source)
XLA Modules:
  0.0 774.8 jit_solution(16630199738598560226)
XLA Ops:
  15.8 51.9 %all_gather.27 = bf16[1024,128]{1,0:T(8,128)(2,1)S(1)} all-gather(bf16[32,128]{1,0:T(8,128)(2,1)} %param.26), channel_id=1, replica_groups=mesh['row'=8,'col'=32] {'col'}, dimensions={0}, use_global_device_ids=true | all-gather | bytes 270336 | tf_op jit(solution)/shard_map/all_gather | solution.py:78
  67.7 47.2 %all_gather.26 = bf16[1024,128]{1,0:T(8,128)(2,1)S(1)} all-gather(bf16[32,128]{1,0:T(8,128)(2,1)} %param.25), channel_id=1, replica_groups=mesh['row'=8,'col'=32] {'col'}, dimensions={0}, use_global_device_ids=true | all-gather | bytes 270336 | tf_op jit(solution)/shard_map/all_gather | solution.py:77
  114.9 47.7 %all_gather.25 = bf16[1024,128]{1,0:T(8,128)(2,1)S(1)} all-gather(bf16[32,128]{1,0:T(8,128)(2,1)} %param.27), channel_id=1, replica_groups=mesh['row'=8,'col'=32] {'col'}, dimensions={0}, use_global_device_ids=true | all-gather | bytes 270336 | tf_op jit(solution)/shard_map/all_gather | solution.py:79
  162.6 51.4 %all_gather.28 = bf16[128,1024]{0,1:T(8,128)(2,1)} all-gather(bf16[128,32]{0,1:T(8,128)(2,1)} %param.28), channel_id=1, replica_groups=mesh['row'=8,'col'=32] {'col'}, dimensions={1}, use_global_device_ids=true | all-gather | bytes 270336 | tf_op jit(solution)/shard_map/all_gather | solution.py:207
  223.5 7.1 all-to-all-start.1
  230.6 8.7 %all-to-all-done.1 = bf16[32,2,384]{2,1,0:T(2,128)(2,1)S(1)} async-done(((bf16[32,2,384]{2,1,0:T(2,128)(2,1)}), bf16[32,2,384]{2,1,0:T(2,128)(2,1)S(1)}, u32[]{:S(2)}, u32[]{:S(2)}) %all-to-all-start.1) | async-done | bytes 49184 | tf_op jit(solution)/shard_map/all_to_all | solution.py:185
  253.0 209.6 %while.14 = (s32[]{:T(128)}, bf16[4,16,128]{2,1,0:T(8,128)(2,1)}, bf16[4,16,2,128,128]{4,3,2,1,0:T(8,128)(2,1)}, s32[4,16,10]{2,1,0:T(8,128)S(1)}, bf16[4,16,384...) while((s32[]{:T(128)}, bf16[4,16,128]{2,1,0:T(8,128)(2,1)}, ...), condition=%wide.region_13.14_spmd, body=%wide.region_10.13_spmd.sunk | while | flops 9330754 | bytes 80879120 | solution.py:192
  273.3 7.3 squeeze.36
  284.3 6.7 copy.137
  291.0 7.3 squeeze.35
  325.7 7.3 squeeze.36
  343.5 7.3 squeeze.35
  378.1 7.3 squeeze.36
  389.1 6.7 copy.137
  395.8 7.3 squeeze.35
  430.4 7.3 squeeze.36
  448.1 7.3 squeeze.35
  470.4 6.9 all-to-all-done.2
  480.2 6.8 all-to-all-start.3
  488.4 58.4 %all-reduce.2.cloned.1.call-done = bf16[528,1024]{1,0:T(8,128)(2,1)} async-done(((bf16[528,1024]{1,0:T(8,128)(2,1)}), bf16[528,1024]{1,0:T(8,128)(2,1)}) %all-reduce.2.cloned.1.call-update) | async-done | bytes 1081360 | tf_op jit(solution)/shard_map/psum | solution.py:211
  548.5 19.2 %all-gather.7.cloned.1.call-done = bf16[1024,512]{1,0:T(8,128)(2,1)} async-done(((bf16[32,512]{1,0:T(8,128)(2,1)}), bf16[1024,512]{1,0:T(8,128)(2,1)}) %all-gather.7.cloned.1.call-update) | async-done | bytes 1048592 | tf_op jit(solution)/shard_map/all_gather | solution.py:217
  571.0 73.5 %all-gather.11.cloned.1.call-done = bf16[512,1024]{0,1:T(8,128)(2,1)} async-done(((bf16[512,32]{0,1:T(8,128)(2,1)}), bf16[512,1024]{0,1:T(8,128)(2,1)}) %all-gather.11.cloned.1.call-update) | async-done | bytes 1048592 | tf_op jit(solution)/shard_map/all_gather | solution.py:226
  644.5 76.8 %all-gather.9.cloned.1.call-done = bf16[1024,512]{1,0:T(8,128)(2,1)} async-done(((bf16[32,512]{1,0:T(8,128)(2,1)}), bf16[1024,512]{1,0:T(8,128)(2,1)}) %all-gather.9.cloned.1.call-update) | async-done | bytes 1048592 | tf_op jit(solution)/shard_map/all_gather | solution.py:218
  729.3 32.6 %reduce-scatter.4.cloned.1.call-done = bf16[128,528]{1,0:T(8,128)(2,1)} async-done(((bf16[1024,528]{1,0:T(8,128)(2,1)}), bf16[128,528]{1,0:T(8,128)(2,1)}) %reduce-scatter.4.cloned.1.call-update) | async-done | bytes 135184
  (249 shorter events, 198.7 us)
Async XLA Ops:
  8.0 210.7 %copy-start.7 = (f32[1024]{0:T(1024)S(1)}, f32[1024]{0:T(1024)}, u32[]{:S(2)}) copy-start(f32[1024]{0:T(1024)} %param.32) | copy-start | bytes 12292
  8.0 209.0 %all-gather.5.cloned.1.call-start = ((), (), s32[]{:S(2)}) async-start(), calls=%async_computation.5 | async-start | bytes 1216512 | tf_op jit(solution)/shard_map/all_gather | solution.py:74
  217.0 3.5 copy-start.2
  221.4 22.9 %copy-start.5 = (f32[2]{0:T(128)S(1)}, f32[2]{0:T(128)}, u32[]{:S(2)}) copy-start(f32[2]{0:T(128)} %param.36) | copy-start | bytes 28
  221.4 22.9 %copy-start.6 = (f32[2]{0:T(128)S(1)}, f32[2]{0:T(128)}, u32[]{:S(2)}) copy-start(f32[2]{0:T(128)} %param.37) | copy-start | bytes 28
  223.5 15.8 %all-to-all-start.1 = ((bf16[32,2,384]{2,1,0:T(2,128)(2,1)}), bf16[32,2,384]{2,1,0:T(2,128)(2,1)S(1)}, u32[]{:S(2)}, u32[]{:S(2)}) async-start(bf16[32,2,384]{2,1,0:T(2,128)(2,1)} %reshape.400), calls=%async_computation.1 | async-start | bytes 98304 | tf_op jit(solution)/shard_map/all_to_all | solution.py:185
  239.3 13.7 %all-to-all-start = ((s32[32,2,10]{2,1,0:T(2,128)}), s32[32,2,10]{2,1,0:T(2,128)S(1)}, u32[]{:S(2)}, u32[]{:S(2)}) async-start(s32[32,2,10]{2,1,0:T(2,128)} %bitcast.30), calls=%async_computation | async-start | bytes 65536 | tf_op jit(solution)/shard_map/all_to_all | solution.py:186
  244.3 8.7 %copy-start = (bf16[32,2,128,128]{3,2,1,0:T(8,128)(2,1)S(1)}, bf16[32,2,128,128]{3,2,1,0:T(8,128)(2,1)}, u32[]{:S(2)}) copy-start(bf16[32,2,128,128]{3,2,1,0:T(8,128)(2,1)} %param.44) | copy-start | bytes 6291460
  244.3 8.7 %copy-start.1 = (s32[32,128]{1,0:T(8,128)S(1)}, s32[32,128]{1,0:T(8,128)}, u32[]{:S(2)}) copy-start(s32[32,128]{1,0:T(8,128)} %param.45) | copy-start | bytes 49156
  462.5 14.8 %all-to-all-start.2 = ((bf16[32,2,128]{2,1,0:T(2,128)(2,1)}), bf16[32,2,128]{2,1,0:T(2,128)(2,1)S(1)}, u32[]{:S(2)}, u32[]{:S(2)}) async-start(bf16[32,2,128]{2,1,0:T(2,128)(2,1)} %bitcast.34), calls=%async_computation.2 | async-start | bytes 32768 | tf_op jit(solution)/shard_map/all_to_all | solution.py:195
  467.6 79.2 %all-reduce.2.cloned.1.call-start = ((), (), s32[]{:S(2)}) async-start(), calls=%async_computation.6 | async-start | bytes 2162688 | tf_op jit(solution)/shard_map/psum | solution.py:211
  467.7 10.4 %copy-start.4 = (bf16[128,1024]{0,1:T(8,128)(2,1)S(1)}, bf16[128,1024]{0,1:T(8,128)(2,1)}, u32[]{:S(2)}) copy-start(bf16[128,1024]{0,1:T(8,128)(2,1)} %all_gather.28) | copy-start | bytes 786436
  479.6 88.1 %all-gather.7.cloned.1.call-start = ((), (), s32[]{:S(2)}) async-start(), calls=%async_computation.7 | async-start | bytes 1081344 | tf_op jit(solution)/shard_map/all_gather | solution.py:217
  480.2 66.7 %copy-start.3 = (bf16[528,1024]{1,0:T(8,128)(2,1)S(1)}, bf16[528,1024]{1,0:T(8,128)(2,1)}, u32[]{:S(2)}) copy-start(bf16[528,1024]{1,0:T(8,128)(2,1)} %all-gather.5.cloned.1.call-done) | copy-start | bytes 3244036
  480.2 283.5 %all-to-all-start.3 = ((bf16[32,2,2,128,128]{4,3,2,1,0:T(8,128)(2,1)}), bf16[32,2,2,128,128]{4,3,2,1,0:T(8,128)(2,1)}, u32[]{:S(2)}, u32[]{:S(2)}) async-start(bf16[32,2,2,128,128]{4,3,2,1,0:T(8,128)(2,1)} %bitcast.142), calls=%async_computation.3 | async-start | bytes 8388608 | tf_op jit(solution)/shard_map/all_to_all | solution.py:198
  487.0 157.5 %all-gather.11.cloned.1.call-start = ((), (), s32[]{:S(2)}) async-start(), calls=%async_computation.9 | async-start | bytes 1081344 | tf_op jit(solution)/shard_map/all_gather | solution.py:226
  487.6 233.7 %all-gather.9.cloned.1.call-start = ((), (), s32[]{:S(2)}) async-start(), calls=%async_computation.8 | async-start | bytes 1081344 | tf_op jit(solution)/shard_map/all_gather | solution.py:218
  488.1 79.6 %copy-start.8 = (f32[1024]{0:T(1024)S(1)}, f32[1024]{0:T(1024)}, u32[]{:S(2)}) copy-start(f32[1024]{0:T(1024)} %param.33) | copy-start | bytes 12292
  488.1 273.8 %reduce-scatter.4.cloned.1.call-start = ((), (), s32[]{:S(2)}) async-start(), calls=%async_computation.10 | async-start | bytes 1474560
Sparse Core Ops, SparseCore 0:
  10.7 28.8 all-gather.4
  479.7 67.0 all-reduce.1
  728.5 33.3 reduce-scatter.3
Sparse Core Ops, SparseCore 1:
  483.0 84.7 all-gather.6
  570.5 73.9 all-gather.10
  647.3 74.0 all-gather.8
where the time goes:
time: 778 us; the launch traced here: 775 us
  waiting for transfers between devices  284 us (37%)
  blocking collectives  198 us (25%)
  local copies, waits for them, and re-layouts  189 us (24%)
  matrix products  42.3 us (5%)
  starting transfers between devices  24.4 us (3%)
  other arithmetic  21.1 us (3%)
  between operations  15.7 us (2%)
    all_gather x1, waiting for transfers between devices, on_device(): lax.all_gather(w_up, 'col', axis=0, tiled=True)  76.8 us
    all_gather x1, waiting for transfers between devices, on_device(): lax.all_gather(w_down, 'col', axis=1, tiled=True)  73.5 us
    psum x1, waiting for transfers between devices, on_device(): lax.psum(partial_out.astype(jnp.bfloat16), 'row').astype(jnp.float32)  58.4 us
    while x8, local copies, waits for them, and re-layouts  53.9 us
    all_gather x1, blocking collectives, on_device(): lax.all_gather(w_k, 'col', axis=0, tiled=True)  51.9 us
    all_gather x1, blocking collectives, on_device(): lax.all_gather(w_o, 'col', axis=1, tiled=True)  51.4 us
    all_gather x1, blocking collectives, on_device(): lax.all_gather(w_v, 'col', axis=0, tiled=True)  47.7 us
    all_gather x1, blocking collectives, on_device(): lax.all_gather(w_q, 'col', axis=0, tiled=True)  47.2 us
  transfers between devices with their start and end apart: 10, of which 8 were waited for; matrix products, arithmetic and copies ran while one was open for 4% of the time, Pallas kernels for 0%

commit v1 on v0

--- a/solution.py
+++ b/solution.py
@@ -74,7 +74,9 @@
     gathered_input = lax.all_gather(layer_input, "row", axis=1, tiled=True)
     normed = norm_rows(gathered_input.astype(jnp.float32), norm1).astype(jnp.bfloat16)
     pieces = (
-        lax.all_gather(w_q, "col", axis=0, tiled=True),
+        jnp.concatenate(
+            lax.all_to_all(jnp.stack([w_q] * lax.axis_size("col")), "col", 0, 0), axis=0
+        ),
         lax.all_gather(w_k, "col", axis=0, tiled=True),
         lax.all_gather(w_v, "col", axis=0, tiled=True),
     )

time: 778 us -> 744 us (0.956)
  blocking collectives: 198 us -> 148 us
  starting transfers between devices: 24.4 us -> 37.9 us
    all_gather x1 -> x0, blocking collectives: 47.2 us -> none  [on_device(): lax.all_gather(w_q, 'col', axis=0, tiled=True)]
    all_to_all x0 -> x1, starting transfers between devices: none -> 11.7 us  [on_device(): lax.all_to_all(jnp.stack([w_q] * lax.axis_size('col')), 'col', 0, 0)]
  transfers between devices with their start and end apart: 10 -> 11, of which waited for: 8 -> 8; matrix products, arithmetic and copies ran while one was open for 4% -> 4% of each run, Pallas kernels for 0% -> 0%
where the time goes in v1:
time: 744 us; the launch traced here: 741 us
  waiting for transfers between devices  285 us (38%)
  local copies, waits for them, and re-layouts  190 us (26%)
  blocking collectives  148 us (20%)
  matrix products  42.3 us (6%)
  starting transfers between devices  37.9 us (5%)
  other arithmetic  21.2 us (3%)
  between operations  15.8 us (2%)
    all_gather x1, waiting for transfers between devices, on_device(): lax.all_gather(w_up, 'col', axis=0, tiled=True)  76.8 us
    all_gather x1, waiting for transfers between devices, on_device(): lax.all_gather(w_down, 'col', axis=1, tiled=True)  73.5 us
    psum x1, waiting for transfers between devices, on_device(): lax.psum(partial_out.astype(jnp.bfloat16), 'row').astype(jnp.float32)  59.3 us
    while x8, local copies, waits for them, and re-layouts  53.9 us
    all_gather x1, blocking collectives, on_device(): lax.all_gather(w_o, 'col', axis=1, tiled=True)  51.7 us
    all_gather x1, blocking collectives, on_device(): lax.all_gather(w_k, 'col', axis=0, tiled=True)  48.6 us
    all_gather x1, blocking collectives, on_device(): lax.all_gather(w_v, 'col', axis=0, tiled=True)  47.3 us
    unnamed x7, waiting for transfers between devices  35 us
  transfers between devices with their start and end apart: 11, of which 8 were waited for; matrix products, arithmetic and copies ran while one was open for 4% of the time, Pallas kernels for 0%

profile of v1, /device:TPU:8, one launch (start us, length us, event | category | flops | bytes accessed | tf_op | source)
XLA Modules:
  0.0 740.9 jit_solution(14996291297350147445)
XLA Ops:
  10.2 11.7 %all-to-all-start = ((bf16[32,32,128]{2,1,0:T(8,128)(2,1)}), bf16[32,32,128]{2,1,0:T(8,128)(2,1)S(1)}, u32[]{:S(2)}, u32[]{:S(2)}) async-start(bf16[32,32,128]{2,1,0:T(8,128)(2,1)} %stack.19), calls=%async_computation | async-start | bytes 524288 | tf_op jit(solution)/shard_map/all_to_all | solution.py:78
  29.0 48.6 %all_gather.23 = bf16[1024,128]{1,0:T(8,128)(2,1)S(1)} all-gather(bf16[32,128]{1,0:T(8,128)(2,1)} %param.26), channel_id=1, replica_groups=mesh['row'=8,'col'=32] {'col'}, dimensions={0}, use_global_device_ids=true | all-gather | bytes 270336 | tf_op jit(solution)/shard_map/all_gather | solution.py:80
  77.6 47.3 %all_gather.22 = bf16[1024,128]{1,0:T(8,128)(2,1)S(1)} all-gather(bf16[32,128]{1,0:T(8,128)(2,1)} %param.27), channel_id=1, replica_groups=mesh['row'=8,'col'=32] {'col'}, dimensions={0}, use_global_device_ids=true | all-gather | bytes 270336 | tf_op jit(solution)/shard_map/all_gather | solution.py:81
  126.4 51.7 %all_gather.24 = bf16[128,1024]{0,1:T(8,128)(2,1)} all-gather(bf16[128,32]{0,1:T(8,128)(2,1)} %param.28), channel_id=1, replica_groups=mesh['row'=8,'col'=32] {'col'}, dimensions={1}, use_global_device_ids=true | all-gather | bytes 270336 | tf_op jit(solution)/shard_map/all_gather | solution.py:209
  186.2 8.2 %all-to-all-start.2 = ((bf16[32,2,384]{2,1,0:T(2,128)(2,1)}), bf16[32,2,384]{2,1,0:T(2,128)(2,1)S(1)}, u32[]{:S(2)}, u32[]{:S(2)}) async-start(bf16[32,2,384]{2,1,0:T(2,128)(2,1)} %reshape.404), calls=%async_computation.2 | async-start | bytes 98304 | tf_op jit(solution)/shard_map/all_to_all | solution.py:187
  194.4 8.7 %all-to-all-done.2 = bf16[32,2,384]{2,1,0:T(2,128)(2,1)S(1)} async-done(((bf16[32,2,384]{2,1,0:T(2,128)(2,1)}), bf16[32,2,384]{2,1,0:T(2,128)(2,1)S(1)}, u32[]{:S(2)}, u32[]{:S(2)}) %all-to-all-start.2) | async-done | bytes 49184 | tf_op jit(solution)/shard_map/all_to_all | solution.py:187
  216.8 209.6 %while.14 = (s32[]{:T(128)}, bf16[4,16,128]{2,1,0:T(8,128)(2,1)}, bf16[4,16,2,128,128]{4,3,2,1,0:T(8,128)(2,1)}, s32[4,16,10]{2,1,0:T(8,128)S(1)}, bf16[4,16,384...) while((s32[]{:T(128)}, bf16[4,16,128]{2,1,0:T(8,128)(2,1)}, ...), condition=%wide.region_13.14_spmd, body=%wide.region_10.13_spmd.sunk | while | flops 9330754 | bytes 80879120 | solution.py:194
  237.1 7.3 squeeze.36
  248.1 6.7 copy.136
  254.8 7.3 squeeze.35
  289.6 7.3 squeeze.36
  300.6 6.7 copy.136
  307.3 7.3 squeeze.35
  341.9 7.3 squeeze.36
  352.9 6.7 copy.136
  359.7 7.3 squeeze.35
  394.3 7.3 squeeze.36
  412.0 7.3 squeeze.35
  443.6 7.5 %all-to-all-start.4 = ((bf16[32,2,2,128,128]{4,3,2,1,0:T(8,128)(2,1)}), bf16[32,2,2,128,128]{4,3,2,1,0:T(8,128)(2,1)}, u32[]{:S(2)}, u32[]{:S(2)}) async-start(bf16[32,2,2,128,128]{4,3,2,1,0:T(8,128)(2,1)} %bitcast.148), calls=%async_computation.4 | async-start | bytes 8388608 | tf_op jit(solution)/shard_map/all_to_all | solution.py:200
  452.5 59.3 %all-reduce.2.cloned.1.call-done = bf16[528,1024]{1,0:T(8,128)(2,1)} async-done(((bf16[528,1024]{1,0:T(8,128)(2,1)}), bf16[528,1024]{1,0:T(8,128)(2,1)}) %all-reduce.2.cloned.1.call-update) | async-done | bytes 1081360 | tf_op jit(solution)/shard_map/psum | solution.py:213
  513.6 20.2 %all-gather.7.cloned.1.call-done = bf16[1024,512]{1,0:T(8,128)(2,1)} async-done(((bf16[32,512]{1,0:T(8,128)(2,1)}), bf16[1024,512]{1,0:T(8,128)(2,1)}) %all-gather.7.cloned.1.call-update) | async-done | bytes 1048592 | tf_op jit(solution)/shard_map/all_gather | solution.py:219
  537.1 73.5 %all-gather.11.cloned.1.call-done = bf16[512,1024]{0,1:T(8,128)(2,1)} async-done(((bf16[512,32]{0,1:T(8,128)(2,1)}), bf16[512,1024]{0,1:T(8,128)(2,1)}) %all-gather.11.cloned.1.call-update) | async-done | bytes 1048592 | tf_op jit(solution)/shard_map/all_gather | solution.py:228
  610.6 76.8 %all-gather.9.cloned.1.call-done = bf16[1024,512]{1,0:T(8,128)(2,1)} async-done(((bf16[32,512]{1,0:T(8,128)(2,1)}), bf16[1024,512]{1,0:T(8,128)(2,1)}) %all-gather.9.cloned.1.call-update) | async-done | bytes 1048592 | tf_op jit(solution)/shard_map/all_gather | solution.py:220
  695.3 32.7 %reduce-scatter.4.cloned.1.call-done = bf16[128,528]{1,0:T(8,128)(2,1)} async-done(((bf16[1024,528]{1,0:T(8,128)(2,1)}), bf16[128,528]{1,0:T(8,128)(2,1)}) %reduce-scatter.4.cloned.1.call-update) | async-done | bytes 135184
  (252 shorter events, 200.1 us)
Async XLA Ops:
  8.0 173.4 %copy-start.7 = (f32[1024]{0:T(1024)S(1)}, f32[1024]{0:T(1024)}, u32[]{:S(2)}) copy-start(f32[1024]{0:T(1024)} %param.32) | copy-start | bytes 12292
  8.0 171.7 %all-gather.5.cloned.1.call-start = ((), (), s32[]{:S(2)}) async-start(), calls=%async_computation.6 | async-start | bytes 1216512 | tf_op jit(solution)/shard_map/all_gather | solution.py:74
  10.2 169.4 %all-to-all-start = ((bf16[32,32,128]{2,1,0:T(8,128)(2,1)}), bf16[32,32,128]{2,1,0:T(8,128)(2,1)S(1)}, u32[]{:S(2)}, u32[]{:S(2)}) async-start(bf16[32,32,128]{2,1,0:T(8,128)(2,1)} %stack.19), calls=%async_computation | async-start | bytes 524288 | tf_op jit(solution)/shard_map/all_to_all | solution.py:78
  179.7 3.5 copy-start.2
  184.1 24.0 %copy-start.5 = (f32[2]{0:T(128)S(1)}, f32[2]{0:T(128)}, u32[]{:S(2)}) copy-start(f32[2]{0:T(128)} %param.36) | copy-start | bytes 28
  184.1 24.0 %copy-start.6 = (f32[2]{0:T(128)S(1)}, f32[2]{0:T(128)}, u32[]{:S(2)}) copy-start(f32[2]{0:T(128)} %param.37) | copy-start | bytes 28
  186.2 16.9 %all-to-all-start.2 = ((bf16[32,2,384]{2,1,0:T(2,128)(2,1)}), bf16[32,2,384]{2,1,0:T(2,128)(2,1)S(1)}, u32[]{:S(2)}, u32[]{:S(2)}) async-start(bf16[32,2,384]{2,1,0:T(2,128)(2,1)} %reshape.404), calls=%async_computation.2 | async-start | bytes 98304 | tf_op jit(solution)/shard_map/all_to_all | solution.py:187
  203.1 13.7 %all-to-all-start.1 = ((s32[32,2,10]{2,1,0:T(2,128)}), s32[32,2,10]{2,1,0:T(2,128)S(1)}, u32[]{:S(2)}, u32[]{:S(2)}) async-start(s32[32,2,10]{2,1,0:T(2,128)} %bitcast.33), calls=%async_computation.1 | async-start | bytes 65536 | tf_op jit(solution)/shard_map/all_to_all | solution.py:188
  208.1 8.7 %copy-start = (bf16[32,2,128,128]{3,2,1,0:T(8,128)(2,1)S(1)}, bf16[32,2,128,128]{3,2,1,0:T(8,128)(2,1)}, u32[]{:S(2)}) copy-start(bf16[32,2,128,128]{3,2,1,0:T(8,128)(2,1)} %param.44) | copy-start | bytes 6291460
  208.1 8.7 %copy-start.1 = (s32[32,128]{1,0:T(8,128)S(1)}, s32[32,128]{1,0:T(8,128)}, u32[]{:S(2)}) copy-start(s32[32,128]{1,0:T(8,128)} %param.45) | copy-start | bytes 49156
  426.4 14.4 %all-to-all-start.3 = ((bf16[32,2,128]{2,1,0:T(2,128)(2,1)}), bf16[32,2,128]{2,1,0:T(2,128)(2,1)S(1)}, u32[]{:S(2)}, u32[]{:S(2)}) async-start(bf16[32,2,128]{2,1,0:T(2,128)(2,1)} %bitcast.37), calls=%async_computation.3 | async-start | bytes 32768 | tf_op jit(solution)/shard_map/all_to_all | solution.py:197
  431.5 80.4 %all-reduce.2.cloned.1.call-start = ((), (), s32[]{:S(2)}) async-start(), calls=%async_computation.7 | async-start | bytes 2162688 | tf_op jit(solution)/shard_map/psum | solution.py:213
  431.5 9.9 %copy-start.4 = (bf16[128,1024]{0,1:T(8,128)(2,1)S(1)}, bf16[128,1024]{0,1:T(8,128)(2,1)}, u32[]{:S(2)}) copy-start(bf16[128,1024]{0,1:T(8,128)(2,1)} %all_gather.24) | copy-start | bytes 786436
  443.0 90.8 %all-gather.7.cloned.1.call-start = ((), (), s32[]{:S(2)}) async-start(), calls=%async_computation.8 | async-start | bytes 1081344 | tf_op jit(solution)/shard_map/all_gather | solution.py:219
  443.6 68.3 %copy-start.3 = (bf16[528,1024]{1,0:T(8,128)(2,1)S(1)}, bf16[528,1024]{1,0:T(8,128)(2,1)}, u32[]{:S(2)}) copy-start(bf16[528,1024]{1,0:T(8,128)(2,1)} %all-gather.5.cloned.1.call-done) | copy-start | bytes 3244036
  443.6 286.2 %all-to-all-start.4 = ((bf16[32,2,2,128,128]{4,3,2,1,0:T(8,128)(2,1)}), bf16[32,2,2,128,128]{4,3,2,1,0:T(8,128)(2,1)}, u32[]{:S(2)}, u32[]{:S(2)}) async-start(bf16[32,2,2,128,128]{4,3,2,1,0:T(8,128)(2,1)} %bitcast.148), calls=%async_computation.4 | async-start | bytes 8388608 | tf_op jit(solution)/shard_map/all_to_all | solution.py:200
  451.1 159.5 %all-gather.11.cloned.1.call-start = ((), (), s32[]{:S(2)}) async-start(), calls=%async_computation.10 | async-start | bytes 1081344 | tf_op jit(solution)/shard_map/all_gather | solution.py:228
  451.7 235.7 %all-gather.9.cloned.1.call-start = ((), (), s32[]{:S(2)}) async-start(), calls=%async_computation.9 | async-start | bytes 1081344 | tf_op jit(solution)/shard_map/all_gather | solution.py:220
  452.3 81.5 %copy-start.8 = (f32[1024]{0:T(1024)S(1)}, f32[1024]{0:T(1024)}, u32[]{:S(2)}) copy-start(f32[1024]{0:T(1024)} %param.33) | copy-start | bytes 12292
  452.3 275.7 %reduce-scatter.4.cloned.1.call-start = ((), (), s32[]{:S(2)}) async-start(), calls=%async_computation.11 | async-start | bytes 1474560
Sparse Core Ops, SparseCore 0:
  10.7 28.8 all-gather.4
  443.1 68.6 all-reduce.1
  694.5 33.4 reduce-scatter.3
Sparse Core Ops, SparseCore 1:
  446.4 87.3 all-gather.6
  536.6 73.9 all-gather.10
  613.3 74.0 all-gather.8
